TPU v7x, 256 devices: a whole 4x4x8 slice. The times are simulated.
256 devices in a mesh: samples: 64 (over z, y, x_lo), vblocks: 4 (over x_hi, core).
Axes of the slice: x: 4 (x_hi: 2, x_lo: 2; x = x_hi * 2 + x_lo), y: 4, z: 8, core: 2. Of those that a mesh axis runs over, the one named last changes fastest.
Arguments:
- genotypes: int32 [65536, 4096], P('samples', 'vblocks'), may hold values from 0 to 2
- typed_mask: int32 [4096], P('vblocks'), may hold values 0 or 1
- z_scores: float32 [1024, 4096], P('samples', 'vblocks'), may hold values from -60 to 60
Outputs:
- solution: float32 [1024, 4096], P('samples', 'vblocks')
- imputed: float32 [1024, 4096], P('samples', 'vblocks')
All inputs are finite; a program needn't handle non-finite values. No bound on the sum of `typed_mask` on one device may be relied on, other than what follows from the above.
Results may differ from a plain program's by a relative error of at most 0.0068.
Values may be sent and summed in bfloat16 or wider, within the bound.
No kernel may reach another device: no remote copies, remote signals or barrier semaphores. Data moves between devices by JAX's collectives and lax.ppermute only.
A program may use at most 64 MiB of HBM per device.

v0:
```python
import jax
import jax.numpy as jnp
from jax import lax
from jax.sharding import PartitionSpec as P

ITERS = 3
RIDGE = 0.1
EPSILON = 1e-05
HIGHEST = lax.Precision.HIGHEST


def passed_along(block, axis, distance):
    devices = range(lax.axis_size(axis))
    route = [(i - distance, i) for i in devices if i - distance in devices]
    return lax.ppermute(block, axis, route)


def contract_rows(first_mat, second_mat):
    return lax.dot_general(
        first_mat, second_mat, (((0,), (0,)), ((), ())), preferred_element_type=jnp.float32
    )


def times_transpose(vector, matrix):
    return lax.dot_general(
        vector,
        matrix,
        (((1,), (1,)), ((), ())),
        precision=HIGHEST,
        preferred_element_type=jnp.float32,
    )


def local_sums(first_vec, second_vec):
    return jnp.sum(first_vec * second_vec, axis=1)


def on_device(genotypes, typed_mask, z_scores):
    samples_dev, block_width = genotypes.shape
    total_samples = samples_dev * lax.axis_size("samples")
    dosage = genotypes.astype(jnp.float32)
    totals, squares = lax.psum(
        (jnp.sum(dosage, axis=0), jnp.sum(dosage * dosage, axis=0)), "samples"
    )
    mean_dosage = totals / total_samples
    variance = squares / total_samples - mean_dosage * mean_dosage
    standard = ((dosage - mean_dosage) * lax.rsqrt(variance + EPSILON)).astype(jnp.bfloat16)
    following = passed_along(standard, "vblocks", -1)
    joined = jnp.concatenate([standard, following], axis=1)
    summed = lax.psum_scatter(
        contract_rows(standard, joined), "samples", scatter_dimension=0, tiled=True
    )
    link_rows = (summed / total_samples).astype(jnp.bfloat16)
    gathered = lax.all_gather(link_rows, "samples", axis=0, tiled=True)
    own_block = gathered[:, :block_width].astype(jnp.float32)
    edge_half = gathered[:, block_width:]
    edge_block = edge_half.astype(jnp.float32)

    def apply_link(vector):
        ahead_part = passed_along(vector, "vblocks", -1)
        outgoing = jnp.dot(
            vector, edge_block, precision=HIGHEST, preferred_element_type=jnp.float32
        )
        lower_part = passed_along(outgoing, "vblocks", 1)
        result = times_transpose(vector, own_block)
        result = result + 0.5 * times_transpose(ahead_part, edge_block)
        return result + 0.5 * lower_part

    mask_row = typed_mask.astype(jnp.float32)[None, :]
    right_side = mask_row * z_scores
    solution = jnp.zeros_like(right_side)
    residual = right_side

    def squares_sum(vector):
        return lax.psum(local_sums(vector, vector), "vblocks")

    direction = right_side
    norm_now = squares_sum(residual)
    for iteration in range(ITERS):
        image = mask_row * apply_link(mask_row * direction) + RIDGE * direction
        step_size = norm_now / lax.psum(local_sums(direction, image), "vblocks")
        solution = solution + step_size[:, None] * direction
        residual = residual - step_size[:, None] * image
        if iteration + 1 < ITERS:
            norm_next = squares_sum(residual)
            direction = residual + (norm_next / norm_now)[:, None] * direction
            norm_now = norm_next
    projected = apply_link(mask_row * solution)
    imputed = jnp.where(typed_mask[None, :] == 1, z_scores, projected)
    return (solution, imputed)


def solution(mesh):
    placed = (P("samples", "vblocks"), P("vblocks"), P("samples", "vblocks"))
    return jax.shard_map(
        on_device,
        mesh=mesh,
        in_specs=placed,
        out_specs=(P("samples", "vblocks"), P("samples", "vblocks")),
        check_vma=False,
    )
```

profile of v0, /device:TPU:1, one launch (start us, length us, event | category | flops | bytes accessed | tf_op | source)
XLA Modules:
  0.0 945.3 jit_solution(10318953864122489320)
XLA Ops:
  7.2 2.8 convert_reduce_fusion
  10.0 136.7 %all-reduce = (f32[1024]{0:T(1024)S(1)}, f32[1024]{0:T(1024)S(1)}) all-reduce(f32[1024]{0:T(1024)S(1)} %get-tuple-element.3, f32[1024]{0:T(1024)S(1)} %get-tuple-element.2), channel_id=1, replica_groups=mesh['samples'=64,'vblocks'=4] {'samples'}, use_global_device_ids=true, to_apply=%region_5.0 | all-reduce | flops 2048 | bytes 16384 | tf_op jit(solution)/shard_map/psum | solution.py:42
  146.7 2.8 multiply_convert_fusion
  149.5 30.3 %collective-permute-start = (bf16[1024,1024]{1,0:T(8,128)(2,1)S(1)}, bf16[1024,1024]{1,0:T(8,128)(2,1)S(1)}, u32[]{:S(2)}, u32[]{:S(2)}) collective-permute-start(bf16[1024,1024]{1,0:T(8,128)(2,1)S(1)} %multiply_convert_fusion), channel_id=1, source_target_pairs={{1,0},{2,1},{3,2},{5,4},{6,5},{7,6},{9,8},{10,9},{11,10},{13,12},{... | collective-permute-start | bytes 6291464 | tf_op jit(solution)/shard_map/ppermute | solution.py:15
  179.9 26.1 %collective-permute-done = bf16[1024,1024]{1,0:T(8,128)(2,1)S(1)} collective-permute-done((bf16[1024,1024]{1,0:T(8,128)(2,1)S(1)}, bf16[1024,1024]{1,0:T(8,128)(2,1)S(1)}, u32[]{:S(2)}, u32[]{:S(2)}) %collective-permute-start) | collective-permute-done | bytes 2097184 | tf_op jit(solution)/shard_map/ppermute | solution.py:15
  206.0 7.0 fusion
  213.1 280.4 %reduce-scatter.2.cloned.1.call-done = f32[16,2048]{1,0:T(8,128)} async-done(((f32[1024,2048]{1,0:T(8,128)}), f32[16,2048]{1,0:T(8,128)}) %reduce-scatter.2.cloned.1.call-update) | async-done | bytes 131088 | tf_op jit(solution)/shard_map/reduce_scatter | solution.py:50
  495.2 50.4 %collective-permute-start.1 = (f32[16,1024]{1,0:T(8,128)S(1)}, f32[16,1024]{1,0:T(8,128)S(1)}, u32[]{:S(2)}, u32[]{:S(2)}) collective-permute-start(f32[16,1024]{1,0:T(8,128)S(1)} %multiply_multiply_fusion), channel_id=1, source_target_pairs={{1,0},{2,1},{3,2},{5,4},{6,5},{7,6},{9,8},{10,9},{11,10},{13,12},{... | collective-permute-start | bytes 196616 | tf_op jit(solution)/shard_map/ppermute | solution.py:15
  545.5 251.5 %all-gather.2.cloned.1.call-done = bf16[1024,2048]{1,0:T(8,128)(2,1)} async-done(((bf16[16,2048]{1,0:T(8,128)(2,1)}), bf16[1024,2048]{1,0:T(8,128)(2,1)}) %all-gather.2.cloned.1.call-update) | async-done | bytes 4194320 | tf_op jit(solution)/shard_map/all_gather | solution.py:54
  797.1 2.7 fusion.38
  799.7 50.3 %collective-permute-start.2 = (f32[16,1024]{1,0:T(8,128)S(1)}, f32[16,1024]{1,0:T(8,128)S(1)}, u32[]{:S(2)}, u32[]{:S(2)}) collective-permute-start(f32[16,1024]{1,0:T(8,128)S(1)} %fusion.38), channel_id=1, source_target_pairs={{0,1},{1,2},{2,3},{4,5},{5,6},{6,7},{8,9},{9,10},{10,11},{12,13},{... | collective-permute-start | bytes 196616 | tf_op jit(solution)/shard_map/ppermute | solution.py:15
  850.1 3.3 fusion.10
  853.4 1.9 multiply_reduce_fusion.4
  855.3 6.6 all-reduce.1
  862.1 7.6 psum.60
  869.8 4.0 collective-permute-start.3
  873.8 2.5 fusion.35
  876.3 3.6 collective-permute-start.4
  879.9 3.3 fusion.8
  885.1 6.6 psum.61
  891.9 7.6 psum.62
  899.6 4.2 collective-permute-start.5
  903.8 2.5 fusion.32
  906.3 3.6 collective-permute-start.6
  909.9 3.3 fusion.6
  913.2 1.9 fusion.28
  915.1 6.6 psum.63
  922.4 3.1 collective-permute-start.7
  925.5 2.5 fusion.29
  928.0 4.7 collective-permute-start.8
  932.7 3.3 fusion.4
  936.0 2.4 fusion.14
  (40 shorter events, 4.9 us)
Async XLA Ops:
  7.2 486.4 %reduce-scatter.2.cloned.1.call-start = ((), (), s32[]{:S(2)}) async-start(), calls=%async_computation.1 | async-start | bytes 8519680 | tf_op jit(solution)/shard_map/reduce_scatter | solution.py:50
  149.5 56.5 %collective-permute-start = (bf16[1024,1024]{1,0:T(8,128)(2,1)S(1)}, bf16[1024,1024]{1,0:T(8,128)(2,1)S(1)}, u32[]{:S(2)}, u32[]{:S(2)}) collective-permute-start(bf16[1024,1024]{1,0:T(8,128)(2,1)S(1)} %multiply_convert_fusion), channel_id=1, source_target_pairs={{1,0},{2,1},{3,2},{5,4},{6,5},{7,6},{9,8},{10,9},{11,10},{13,12},{... | collective-permute-start | bytes 6291464 | tf_op jit(solution)/shard_map/ppermute | solution.py:15
  213.0 282.1 %copy-start.5 = (s32[1024]{0:T(1024)S(1)}, s32[1024]{0:T(1024)}, u32[]{:S(2)}) copy-start(s32[1024]{0:T(1024)} %param.4) | copy-start | bytes 12292
  213.0 282.1 %copy-start.4 = (f32[16,1024]{1,0:T(8,128)S(1)}, f32[16,1024]{1,0:T(8,128)}, u32[]{:S(2)}) copy-start(f32[16,1024]{1,0:T(8,128)} %param.5) | copy-start | bytes 196612
  213.0 584.0 %all-gather.2.cloned.1.call-start = ((), (), s32[]{:S(2)}) async-start(), calls=%async_computation.2 | async-start | bytes 4259840 | tf_op jit(solution)/shard_map/all_gather | solution.py:54
  495.2 358.2 %collective-permute-start.1 = (f32[16,1024]{1,0:T(8,128)S(1)}, f32[16,1024]{1,0:T(8,128)S(1)}, u32[]{:S(2)}, u32[]{:S(2)}) collective-permute-start(f32[16,1024]{1,0:T(8,128)S(1)} %multiply_multiply_fusion), channel_id=1, source_target_pairs={{1,0},{2,1},{3,2},{5,4},{6,5},{7,6},{9,8},{10,9},{11,10},{13,12},{... | collective-permute-start | bytes 196616 | tf_op jit(solution)/shard_map/ppermute | solution.py:15
  797.0 56.4 %copy-start = (bf16[1024,2048]{1,0:T(8,128)(2,1)S(1)}, bf16[1024,2048]{1,0:T(8,128)(2,1)}, u32[]{:S(2)}) copy-start(bf16[1024,2048]{1,0:T(8,128)(2,1)} %all-gather.2.cloned.1.call-done) | copy-start | bytes 12582916
  799.7 53.7 %collective-permute-start.2 = (f32[16,1024]{1,0:T(8,128)S(1)}, f32[16,1024]{1,0:T(8,128)S(1)}, u32[]{:S(2)}, u32[]{:S(2)}) collective-permute-start(f32[16,1024]{1,0:T(8,128)S(1)} %fusion.38), channel_id=1, source_target_pairs={{0,1},{1,2},{2,3},{4,5},{5,6},{6,7},{8,9},{9,10},{10,11},{12,13},{... | collective-permute-start | bytes 196616 | tf_op jit(solution)/shard_map/ppermute | solution.py:15
  869.7 13.6 %copy-start.1 = (bf16[1024,2048]{1,0:T(8,128)(2,1)S(1)}, bf16[1024,2048]{1,0:T(8,128)(2,1)}, u32[]{:S(2)}) copy-start(bf16[1024,2048]{1,0:T(8,128)(2,1)} %all-gather.2.cloned.1.call-done) | copy-start | bytes 12582916
  869.8 13.4 %collective-permute-start.3 = (f32[16,1024]{1,0:T(8,128)S(1)}, f32[16,1024]{1,0:T(8,128)S(1)}, u32[]{:S(2)}, u32[]{:S(2)}) collective-permute-start(f32[16,1024]{1,0:T(8,128)S(1)} %get-tuple-element.14), channel_id=1, source_target_pairs={{1,0},{2,1},{3,2},{5,4},{6,5},{7,6},{9,8},{10,9},{11,10},{13,12},{... | collective-permute-start | bytes 196616 | tf_op jit(solution)/shard_map/ppermute | solution.py:15
  876.3 6.9 collective-permute-start.4
  899.5 13.7 %copy-start.2 = (bf16[1024,2048]{1,0:T(8,128)(2,1)S(1)}, bf16[1024,2048]{1,0:T(8,128)(2,1)}, u32[]{:S(2)}) copy-start(bf16[1024,2048]{1,0:T(8,128)(2,1)} %all-gather.2.cloned.1.call-done) | copy-start | bytes 12582916
  899.6 13.6 %collective-permute-start.5 = (f32[16,1024]{1,0:T(8,128)S(1)}, f32[16,1024]{1,0:T(8,128)S(1)}, u32[]{:S(2)}, u32[]{:S(2)}) collective-permute-start(f32[16,1024]{1,0:T(8,128)S(1)} %get-tuple-element.12), channel_id=1, source_target_pairs={{1,0},{2,1},{3,2},{5,4},{6,5},{7,6},{9,8},{10,9},{11,10},{13,12},{... | collective-permute-start | bytes 196616 | tf_op jit(solution)/shard_map/ppermute | solution.py:15
  906.3 6.9 collective-permute-start.6
  921.7 14.3 %copy-start.3 = (bf16[1024,2048]{1,0:T(8,128)(2,1)S(1)}, bf16[1024,2048]{1,0:T(8,128)(2,1)}, u32[]{:S(2)}) copy-start(bf16[1024,2048]{1,0:T(8,128)(2,1)} %all-gather.2.cloned.1.call-done) | copy-start | bytes 12582916
  922.4 13.6 %collective-permute-start.7 = (f32[16,1024]{1,0:T(8,128)S(1)}, f32[16,1024]{1,0:T(8,128)S(1)}, u32[]{:S(2)}, u32[]{:S(2)}) collective-permute-start(f32[16,1024]{1,0:T(8,128)S(1)} %get-tuple-element.10), channel_id=1, source_target_pairs={{1,0},{2,1},{3,2},{5,4},{6,5},{7,6},{9,8},{10,9},{11,10},{13,12},{... | collective-permute-start | bytes 196616 | tf_op jit(solution)/shard_map/ppermute | solution.py:15
  928.0 8.0 collective-permute-start.8
Sparse Core Ops, SparseCore 0:
  213.2 280.3 reduce-scatter.1
  495.9 301.1 all-gather.1
where the time goes:
time: 946 us; the launch traced here: 945 us
  waiting for transfers between devices  558 us (59%)
  blocking collectives  172 us (18%)
  starting transfers between devices  154 us (16%)
  matrix products  38.4 us (4%)
  between operations  14.3 us (2%)
    reduce_scatter x1, waiting for transfers between devices, on_device(): lax.psum_scatter(contract_rows(standard, joined), 'samples', scatter_dime...  280 us
    all_gather x1, waiting for transfers between devices, on_device(): gathered = lax.all_gather(link_rows, 'samples', axis=0, tiled=True)  252 us
    ppermute x9, starting transfers between devices, passed_along(): return lax.ppermute(block, axis, route)  154 us
    psum x1, blocking collectives, on_device(): lax.psum((jnp.sum(dosage, axis=0), jnp.sum(dosage * dosage, axis=0)), 'sa...  137 us
    ppermute x9, waiting for transfers between devices, passed_along(): return lax.ppermute(block, axis, route)  26.2 us
    psum x3, blocking collectives, squares_sum(): return lax.psum(local_sums(vector, vector), 'vblocks')  21.8 us
    dot_general x8, matrix products, times_transpose(): lax.dot_general(vector, matrix, (((1,), (1,)), ((), ())), precision=HIGHE...  21.2 us
  transfers between devices with their start and end apart: 11, of which 3 were waited for; matrix products, arithmetic and copies ran while one was open for 2% of the time, Pallas kernels for 0%

commit v1 on v0

--- a/solution.py
+++ b/solution.py
@@ -51,7 +51,10 @@
         contract_rows(standard, joined), "samples", scatter_dimension=0, tiled=True
     )
     link_rows = (summed / total_samples).astype(jnp.bfloat16)
-    gathered = lax.all_gather(link_rows, "samples", axis=0, tiled=True)
+    size = lax.axis_size("samples")
+    blocks = jnp.stack([link_rows for _ in range(size)])
+    blocks = lax.all_to_all(blocks, "samples", split_axis=0, concat_axis=0)
+    gathered = jnp.concatenate(blocks, axis=0)
     own_block = gathered[:, :block_width].astype(jnp.float32)
     edge_half = gathered[:, block_width:]
     edge_block = edge_half.astype(jnp.float32)

time: 946 us -> 722 us (0.76)
  waiting for transfers between devices: 558 us -> 308 us
  starting transfers between devices: 154 us -> 172 us
    all_gather x1 -> x0, waiting for transfers between devices: 252 us -> none  [on_device(): gathered = lax.all_gather(link_rows, 'samples', axis=0, tiled=True)]
    ppermute x9, starting transfers between devices: 154 us -> 166 us  [passed_along(): return lax.ppermute(block, axis, route)]
  transfers between devices with their start and end apart: 11 -> 11, of which waited for: 3 -> 2; matrix products, arithmetic and copies ran while one was open for 2% -> 2% of each run, Pallas kernels for 0% -> 0%
where the time goes in v1:
time: 722 us; the launch traced here: 721 us
  waiting for transfers between devices  308 us (43%)
  starting transfers between devices  172 us (24%)
  blocking collectives  172 us (24%)
  matrix products  44.6 us (6%)
  between operations  14.3 us (2%)
  other arithmetic  7.86 us (1%)
    reduce_scatter x1, waiting for transfers between devices, on_device(): lax.psum_scatter(contract_rows(standard, joined), 'samples', scatter_dime...  282 us
    ppermute x9, starting transfers between devices, passed_along(): return lax.ppermute(block, axis, route)  166 us
    psum x1, blocking collectives, on_device(): lax.psum((jnp.sum(dosage, axis=0), jnp.sum(dosage * dosage, axis=0)), 'sa...  137 us
    dot_general x8, matrix products, times_transpose(): lax.dot_general(vector, matrix, (((1,), (1,)), ((), ())), precision=HIGHE...  27.6 us
    ppermute x9, waiting for transfers between devices, passed_along(): return lax.ppermute(block, axis, route)  26.2 us
    psum x3, blocking collectives, squares_sum(): return lax.psum(local_sums(vector, vector), 'vblocks')  21.8 us
  transfers between devices with their start and end apart: 11, of which 2 were waited for; matrix products, arithmetic and copies ran while one was open for 2% of the time, Pallas kernels for 0%

profile of v1, /device:TPU:1, one launch (start us, length us, event | category | flops | bytes accessed | tf_op | source)
XLA Modules:
  0.0 721.0 jit_solution(14772173988426731205)
XLA Ops:
  7.2 2.8 convert_reduce_fusion
  10.0 136.7 %all-reduce = (f32[1024]{0:T(1024)S(1)}, f32[1024]{0:T(1024)S(1)}) all-reduce(f32[1024]{0:T(1024)S(1)} %get-tuple-element.3, f32[1024]{0:T(1024)S(1)} %get-tuple-element.2), channel_id=1, replica_groups=mesh['samples'=64,'vblocks'=4] {'samples'}, use_global_device_ids=true, to_apply=%region_5.0 | all-reduce | flops 2048 | bytes 16384 | tf_op jit(solution)/shard_map/psum | solution.py:42
  146.7 2.8 multiply_convert_fusion
  149.5 30.3 %collective-permute-start = (bf16[1024,1024]{1,0:T(8,128)(2,1)S(1)}, bf16[1024,1024]{1,0:T(8,128)(2,1)S(1)}, u32[]{:S(2)}, u32[]{:S(2)}) collective-permute-start(bf16[1024,1024]{1,0:T(8,128)(2,1)S(1)} %multiply_convert_fusion), channel_id=1, source_target_pairs={{1,0},{2,1},{3,2},{5,4},{6,5},{7,6},{9,8},{10,9},{11,10},{13,12},{... | collective-permute-start | bytes 6291464 | tf_op jit(solution)/shard_map/ppermute | solution.py:15
  179.9 26.1 %collective-permute-done = bf16[1024,1024]{1,0:T(8,128)(2,1)S(1)} collective-permute-done((bf16[1024,1024]{1,0:T(8,128)(2,1)S(1)}, bf16[1024,1024]{1,0:T(8,128)(2,1)S(1)}, u32[]{:S(2)}, u32[]{:S(2)}) %collective-permute-start) | collective-permute-done | bytes 2097184 | tf_op jit(solution)/shard_map/ppermute | solution.py:15
  206.0 7.0 fusion
  213.0 281.8 %reduce-scatter.2.cloned.1.call-done = f32[16,2048]{1,0:T(8,128)} async-done(((f32[1024,2048]{1,0:T(8,128)}), f32[16,2048]{1,0:T(8,128)}) %reduce-scatter.2.cloned.1.call-update) | async-done | bytes 131088 | tf_op jit(solution)/shard_map/reduce_scatter | solution.py:50
  498.2 5.8 all-to-all-start
  504.1 58.0 %collective-permute-start.1 = (f32[16,1024]{1,0:T(8,128)S(1)}, f32[16,1024]{1,0:T(8,128)S(1)}, u32[]{:S(2)}, u32[]{:S(2)}) collective-permute-start(f32[16,1024]{1,0:T(8,128)S(1)} %multiply_multiply_fusion), channel_id=1, source_target_pairs={{1,0},{2,1},{3,2},{5,4},{6,5},{7,6},{9,8},{10,9},{11,10},{13,12},{... | collective-permute-start | bytes 196616 | tf_op jit(solution)/shard_map/ppermute | solution.py:15
  562.1 2.5 fusion.38
  564.6 55.5 %collective-permute-start.2 = (f32[16,1024]{1,0:T(8,128)S(1)}, f32[16,1024]{1,0:T(8,128)S(1)}, u32[]{:S(2)}, u32[]{:S(2)}) collective-permute-start(f32[16,1024]{1,0:T(8,128)S(1)} %fusion.38), channel_id=1, source_target_pairs={{0,1},{1,2},{2,3},{4,5},{5,6},{6,7},{8,9},{9,10},{10,11},{12,13},{... | collective-permute-start | bytes 196616 | tf_op jit(solution)/shard_map/ppermute | solution.py:15
  620.1 3.3 fusion.10
  623.5 3.4 multiply_reduce_fusion.4
  626.9 6.6 all-reduce.1
  633.8 7.6 %psum.60 = f32[16]{0:T(128)S(1)} all-reduce(f32[16]{0:T(128)S(1)} %get-tuple-element.16), channel_id=1, replica_groups=mesh['samples'=64,'vblocks'=4] {'vblocks'}, use_global_device_ids=true, to_apply=%region_10.0 | all-reduce | flops 16 | bytes 128 | tf_op jit(solution)/shard_map/psum | solution.py:78
  641.4 2.5 fusion.35
  643.9 3.7 collective-permute-start.3
  647.7 3.8 collective-permute-start.4
  651.4 3.3 fusion.8
  654.8 3.4 multiply_reduce_fusion.2
  658.2 6.6 psum.61
  665.1 7.6 %psum.62 = f32[16]{0:T(128)S(1)} all-reduce(f32[16]{0:T(128)S(1)} %multiply_reduce_fusion.1), channel_id=1, replica_groups=mesh['samples'=64,'vblocks'=4] {'vblocks'}, use_global_device_ids=true, to_apply=%region_14.0 | all-reduce | flops 16 | bytes 128 | tf_op jit(solution)/shard_map/psum | solution.py:78
  672.7 2.5 fusion.32
  675.3 3.6 collective-permute-start.5
  678.8 3.8 collective-permute-start.6
  682.6 3.3 fusion.6
  685.9 3.4 fusion.28
  689.4 6.6 psum.63
  699.2 2.9 collective-permute-start.7
  702.2 4.7 collective-permute-start.8
  706.9 3.3 fusion.4
  710.2 4.0 fusion.14
  (32 shorter events, 7.4 us)
Async XLA Ops:
  7.2 487.7 %reduce-scatter.2.cloned.1.call-start = ((), (), s32[]{:S(2)}) async-start(), calls=%async_computation.2 | async-start | bytes 8519680 | tf_op jit(solution)/shard_map/reduce_scatter | solution.py:50
  149.5 56.5 %collective-permute-start = (bf16[1024,1024]{1,0:T(8,128)(2,1)S(1)}, bf16[1024,1024]{1,0:T(8,128)(2,1)S(1)}, u32[]{:S(2)}, u32[]{:S(2)}) collective-permute-start(bf16[1024,1024]{1,0:T(8,128)(2,1)S(1)} %multiply_convert_fusion), channel_id=1, source_target_pairs={{1,0},{2,1},{3,2},{5,4},{6,5},{7,6},{9,8},{10,9},{11,10},{13,12},{... | collective-permute-start | bytes 6291464 | tf_op jit(solution)/shard_map/ppermute | solution.py:15
  498.2 5.8 copy-start.1
  498.2 5.8 copy-start
  498.2 63.9 %all-to-all-start = ((bf16[64,16,2048]{2,1,0:T(8,128)(2,1)}), bf16[64,16,2048]{2,1,0:T(8,128)(2,1)}, u32[]{:S(2)}, u32[]{:S(2)}) async-start(bf16[64,16,2048]{2,1,0:T(8,128)(2,1)} %stack.2), calls=%async_computation.1 | async-start | bytes 8388608 | tf_op jit(solution)/shard_map/all_to_all | solution.py:56
  504.1 119.4 %collective-permute-start.1 = (f32[16,1024]{1,0:T(8,128)S(1)}, f32[16,1024]{1,0:T(8,128)S(1)}, u32[]{:S(2)}, u32[]{:S(2)}) collective-permute-start(f32[16,1024]{1,0:T(8,128)S(1)} %multiply_multiply_fusion), channel_id=1, source_target_pairs={{1,0},{2,1},{3,2},{5,4},{6,5},{7,6},{9,8},{10,9},{11,10},{13,12},{... | collective-permute-start | bytes 196616 | tf_op jit(solution)/shard_map/ppermute | solution.py:15
  564.6 58.8 %collective-permute-start.2 = (f32[16,1024]{1,0:T(8,128)S(1)}, f32[16,1024]{1,0:T(8,128)S(1)}, u32[]{:S(2)}, u32[]{:S(2)}) collective-permute-start(f32[16,1024]{1,0:T(8,128)S(1)} %fusion.38), channel_id=1, source_target_pairs={{0,1},{1,2},{2,3},{4,5},{5,6},{6,7},{8,9},{9,10},{10,11},{12,13},{... | collective-permute-start | bytes 196616 | tf_op jit(solution)/shard_map/ppermute | solution.py:15
  643.9 10.8 %collective-permute-start.3 = (f32[16,1024]{1,0:T(8,128)S(1)}, f32[16,1024]{1,0:T(8,128)S(1)}, u32[]{:S(2)}, u32[]{:S(2)}) collective-permute-start(f32[16,1024]{1,0:T(8,128)S(1)} %get-tuple-element.14), channel_id=1, source_target_pairs={{1,0},{2,1},{3,2},{5,4},{6,5},{7,6},{9,8},{10,9},{11,10},{13,12},{... | collective-permute-start | bytes 196616 | tf_op jit(solution)/shard_map/ppermute | solution.py:15
  647.7 7.1 collective-permute-start.4
  675.3 10.7 %collective-permute-start.5 = (f32[16,1024]{1,0:T(8,128)S(1)}, f32[16,1024]{1,0:T(8,128)S(1)}, u32[]{:S(2)}, u32[]{:S(2)}) collective-permute-start(f32[16,1024]{1,0:T(8,128)S(1)} %get-tuple-element.12), channel_id=1, source_target_pairs={{1,0},{2,1},{3,2},{5,4},{6,5},{7,6},{9,8},{10,9},{11,10},{13,12},{... | collective-permute-start | bytes 196616 | tf_op jit(solution)/shard_map/ppermute | solution.py:15
  678.8 7.1 collective-permute-start.6
  699.2 11.0 %collective-permute-start.7 = (f32[16,1024]{1,0:T(8,128)S(1)}, f32[16,1024]{1,0:T(8,128)S(1)}, u32[]{:S(2)}, u32[]{:S(2)}) collective-permute-start(f32[16,1024]{1,0:T(8,128)S(1)} %get-tuple-element.10), channel_id=1, source_target_pairs={{1,0},{2,1},{3,2},{5,4},{6,5},{7,6},{9,8},{10,9},{11,10},{13,12},{... | collective-permute-start | bytes 196616 | tf_op jit(solution)/shard_map/ppermute | solution.py:15
  702.2 8.0 %collective-permute-start.8 = (f32[16,1024]{1,0:T(8,128)S(1)}, f32[16,1024]{1,0:T(8,128)S(1)}, u32[]{:S(2)}, u32[]{:S(2)}) collective-permute-start(f32[16,1024]{1,0:T(8,128)S(1)} %fusion.29), channel_id=1, source_target_pairs={{0,1},{1,2},{2,3},{4,5},{5,6},{6,7},{8,9},{9,10},{10,11},{12,13},{... | collective-permute-start | bytes 196616 | tf_op jit(solution)/shard_map/ppermute | solution.py:15
Sparse Core Ops, SparseCore 0:
  213.1 281.6 reduce-scatter.1
